TPU v7x, 512 devices: a whole 4x8x8 slice. The times are simulated.
512 devices in a mesh: mp: 8 (over z), section: 4 (over x_hi, core), dp: 16 (over y, x_lo).
Axes of the slice: x: 4 (x_hi: 2, x_lo: 2; x = x_hi * 2 + x_lo), y: 8, z: 8, core: 2. Of those that a mesh axis runs over, the one named last changes fastest.
Arguments:
- residual_in: float32 [4, 5120, 1024], P('section', ('dp', 'mp')), parts along dimension 1
- pre_activation: bfloat16 [4, 5120, 8192], P('section', 'dp', 'mp'), parts along dimension 1, may hold values from -6 to 6
- down_projection: bfloat16 [4, 8192, 1024], P('section', 'mp'), may hold values from -0.0625 to 0.0625
- attention_gain: float32 [4, 1024], P('section'), may hold values from 0.1 to 1.9
- qkv_projection: bfloat16 [4, 1024, 16, 384], P('section', None, 'mp'), may hold values from -0.1875 to 0.1875
- layer_counts: int32 [4], P('section'), may hold values from 1 to 8
Outputs:
- finished_stream: float32 [4, 5120, 1024], P('section', ('dp', 'mp')), parts along dimension 1
- qkv_heads: bfloat16 [4, 5120, 16, 384], P('section', 'dp', 'mp'), parts along dimension 1
There are 16 independent parts, one for each index of `dp`. A program takes and returns all parts, laid end to end along the dimension named above; an argument that names none is the same for every part. Nothing has to cross between parts.
All inputs are finite; a program needn't handle non-finite values.
Results may differ from a plain program's by a relative error of at most 0.001.
The roundings to bfloat16 on the way count: a program that leaves them out, or rounds other values in their place, can miss the bound.
Values may be sent and summed in bfloat16 or wider, within the bound.
A program may use at most 64 MiB of HBM per device.

v0:
```python
import jax
import jax.numpy as jnp
from jax import lax
from jax.sharding import PartitionSpec as P


def gathered_total(value, axis):
    parts = lax.all_gather(value, axis)
    return parts.sum(axis=0)


def cut_along(value, dim, size):
    before, after = (value.shape[:dim], value.shape[dim + 1 :])
    return jnp.moveaxis(value.reshape(*before, size, -1, *after), dim, 0)


def sent_and_summed(value, axis, dim):
    size = lax.axis_size(axis)
    parts = lax.all_to_all(cut_along(value, dim, size), axis, 0, 0, tiled=True)
    return jnp.sum(parts, axis=0)


def passed_along(value, axis, by):
    size = lax.axis_size(axis)
    return lax.ppermute(value, axis, [(i, (i + by) % size) for i in range(size)])


def joined_along(parts, dim):
    parts = jnp.moveaxis(parts, 0, dim)
    dims = parts.shape
    return parts.reshape(*dims[:dim], dims[dim] * dims[dim + 1], *dims[dim + 2 :])


def sent_to_all(value, axis):
    copies = jnp.broadcast_to(value, (lax.axis_size(axis), *value.shape))
    return lax.all_to_all(copies, axis, split_axis=0, concat_axis=0, tiled=True)


def gathered_copies(value, axis, dim):
    return joined_along(sent_to_all(value, axis), dim)


def body(
    residual_in, pre_activation, down_projection, attention_gain, qkv_projection, layer_counts
):
    depth_total = gathered_total(layer_counts, "section")
    branch_scale = 1.0 / jnp.sqrt(depth_total.astype(jnp.float32))[0]
    hidden = jnp.maximum(pre_activation[0], jnp.zeros((), pre_activation.dtype))
    weight = down_projection[0]
    gain_row = attention_gain[0]
    qkv_matrix = qkv_projection[0].reshape(qkv_projection.shape[1], -1)
    finished = (
        sent_and_summed(
            jnp.dot(hidden, weight, preferred_element_type=jnp.float32) * branch_scale, "mp", 0
        )
        + residual_in[0]
    )
    incoming = passed_along(finished, "section", 1)
    mean_square = jnp.mean(incoming * incoming, axis=-1, keepdims=True)
    normed = (incoming * lax.rsqrt(mean_square + 1e-06) * gain_row).astype(jnp.bfloat16)
    product = jnp.dot(
        gathered_copies(normed, "mp", 0), qkv_matrix, preferred_element_type=jnp.float32
    ).astype(jnp.bfloat16)
    qkv_heads = product.reshape(
        1, product.shape[0], qkv_projection.shape[2], qkv_projection.shape[3]
    )
    return (finished[None], qkv_heads)


def solution(mesh):
    return jax.shard_map(
        body,
        mesh=mesh,
        in_specs=(
            P("section", ("dp", "mp"), None),
            P("section", "dp", "mp"),
            P("section", "mp", None),
            P("section", None),
            P("section", None, "mp", None),
            P("section"),
        ),
        out_specs=(P("section", ("dp", "mp"), None), P("section", "dp", "mp", None)),
        check_vma=False,
    )
```

profile of v0, /device:TPU:1, one launch (start us, length us, event | category | flops | bytes accessed | tf_op | source)
XLA Modules:
  0.0 91.8 jit_solution(8951116548059236250)
XLA Ops:
  0.6 0.0 copy-start
  1.4 1.3 %dynamic-slice = u32[1]{0:T(128)} dynamic-slice(u32[512]{0:T(512)} %constant.21, u32[]{:T(128)S(6)} %add.21), dynamic_slice_sizes={1} | dynamic-slice | bytes 12
  2.7 0.8 dynamic-update-slice
  3.5 8.9 %all-reduce = s32[4]{0:T(128)S(1)} all-reduce(s32[4]{0:T(128)S(1)} %dynamic-update-slice), channel_id=2, replica_groups=mesh['mp'=8,'section'=4,'dp'=16] {'section'}, use_global_device_ids=true, to_apply=%add | all-reduce | flops 4 | bytes 32
  12.4 0.6 reduce.1
  13.7 0.0 copy-done
  13.7 1.9 %fusion.2 = f32[320,1024]{1,0:T(8,128)S(1)} fusion(bf16[1,1024,1024]{2,1,0:T(8,128)(2,1)S(1)} %copy-done, f32[]{:T(128)S(6)} %sqrt.3, bf16[1,320,1024]{2,1,0:T(8,128)(2,1)} %param.7), kind=kOutput, calls=%fused_computation.2 | convolution fusion | flops 671744000 | bytes 4063236 | tf_op jit(solution)/shard_map/dot_general | solution.py:54
  15.7 39.5 %all_to_all.10 = f32[8,40,1024]{2,1,0:T(8,128)S(1)} all-to-all(f32[8,40,1024]{2,1,0:T(8,128)S(1)} %bitcast.23), channel_id=1, replica_groups=mesh['mp'=8,'section'=4,'dp'=16] {'mp'}, dimensions={0} | all-to-all | bytes 2621440 | tf_op jit(solution)/shard_map/all_to_all | solution.py:19
  55.2 0.0 copy-start.3
  55.2 0.7 reduce_sum.30
  56.0 1.0 %bitcast_add_fusion = f32[40,1024]{1,0:T(8,128)S(1)} fusion(f32[40,1024]{1,0:T(8,128)} %reduce_sum.30, f32[1,40,1024]{2,1,0:T(8,128)} %param.6), kind=kLoop, calls=%fused_computation.7 | loop fusion | flops 40960 | bytes 491520 | tf_op jit(solution)/shard_map/add | solution.py:53
  57.0 6.6 %collective-permute-start = (f32[40,1024]{1,0:T(8,128)S(1)}, f32[40,1024]{1,0:T(8,128)S(1)}, u32[]{:S(2)}, u32[]{:S(2)}) collective-permute-start(f32[40,1024]{1,0:T(8,128)S(1)} %bitcast_add_fusion), channel_id=1, source_target_pairs={{0,16},{16,32},{32,48},{48,0},{1,17},{17,33},{33,49},{49,1},{2,18}... | collective-permute-start | bytes 491528 | tf_op jit(solution)/shard_map/ppermute | solution.py:25
  63.6 2.2 %collective-permute-done = f32[40,1024]{1,0:T(8,128)S(1)} collective-permute-done((f32[40,1024]{1,0:T(8,128)S(1)}, f32[40,1024]{1,0:T(8,128)S(1)}, u32[]{:S(2)}, u32[]{:S(2)}) %collective-permute-start) | collective-permute-done | bytes 163872 | tf_op jit(solution)/shard_map/ppermute | solution.py:25
  65.9 0.1 multiply_reduce_fusion
  66.0 0.0 copy-done.3
  66.0 0.1 multiply_convert_fusion
  66.1 0.9 %broadcast_in_dim.2 = bf16[8,40,1024]{2,1,0:T(8,128)(2,1)} broadcast(bf16[40,1024]{1,0:T(8,128)(2,1)S(1)} %multiply_convert_fusion), dimensions={1,2} | broadcast | bytes 737280 | tf_op jit(solution)/shard_map/broadcast_in_dim | solution.py:35
  67.0 3.5 %all-to-all-start.1 = ((bf16[8,40,1024]{2,1,0:T(8,128)(2,1)}), bf16[8,40,1024]{2,1,0:T(8,128)(2,1)S(1)}, u32[]{:S(2)}, u32[]{:S(2)}) async-start(bf16[8,40,1024]{2,1,0:T(8,128)(2,1)} %broadcast_in_dim.2), calls=%async_computation.1 | async-start | bytes 1310720 | tf_op jit(solution)/shard_map/all_to_all | solution.py:36
  70.6 0.0 copy-start.1
  70.6 0.0 copy-start.2
  70.6 2.9 %copy.8 = bf16[128,8,2,384]{3,1,2,0:T(8,128)(2,1)} copy(bf16[128,8,2,384]{3,2,1,0:T(2,128)(2,1)} %bitcast.21) | data formatting | bytes 3145728
  73.5 0.0 copy-done.1
  73.5 0.0 copy-done.2
  73.5 0.7 bitcast_add_fusion.1
  74.2 14.6 %all-to-all-done.1 = bf16[8,40,1024]{2,1,0:T(8,128)(2,1)S(1)} async-done(((bf16[8,40,1024]{2,1,0:T(8,128)(2,1)}), bf16[8,40,1024]{2,1,0:T(8,128)(2,1)S(1)}, u32[]{:S(2)}, u32[]{:S(2)}) %all-to-all-start.1) | async-done | bytes 655392 | tf_op jit(solution)/shard_map/all_to_all | solution.py:36
  88.8 2.1 %convolution_convert_fusion = bf16[320,768]{1,0:T(8,128)(2,1)S(1)} fusion(bf16[320,1024]{1,0:T(8,128)(2,1)S(1)} %bitcast.24, bf16[1024,768]{1,0:T(8,128)(2,1)} %bitcast.22), kind=kOutput, calls=%fused_computation.3 | convolution fusion | flops 503562240 | bytes 2719744 | tf_op jit(solution)/shard_map/dot_general | solution.py:61
  90.9 0.9 reshape.31
  (2 shorter events, 0.0 us)
Async XLA Ops:
  0.6 13.1 %copy-start = (bf16[1,1024,1024]{2,1,0:T(8,128)(2,1)S(1)}, bf16[1,1024,1024]{2,1,0:T(8,128)(2,1)}, u32[]{:S(2)}) copy-start(bf16[1,1024,1024]{2,1,0:T(8,128)(2,1)} %param.8) | copy-start | bytes 6291460
  55.2 10.8 %copy-start.3 = (f32[1,1024]{1,0:T(1,128)S(1)}, f32[1,1024]{1,0:T(1,128)}, u32[]{:S(2)}) copy-start(f32[1,1024]{1,0:T(1,128)} %param.9) | copy-start | bytes 12292
  57.0 8.9 %collective-permute-start = (f32[40,1024]{1,0:T(8,128)S(1)}, f32[40,1024]{1,0:T(8,128)S(1)}, u32[]{:S(2)}, u32[]{:S(2)}) collective-permute-start(f32[40,1024]{1,0:T(8,128)S(1)} %bitcast_add_fusion), channel_id=1, source_target_pairs={{0,16},{16,32},{32,48},{48,0},{1,17},{17,33},{33,49},{49,1},{2,18}... | collective-permute-start | bytes 491528 | tf_op jit(solution)/shard_map/ppermute | solution.py:25
  67.0 21.8 %all-to-all-start.1 = ((bf16[8,40,1024]{2,1,0:T(8,128)(2,1)}), bf16[8,40,1024]{2,1,0:T(8,128)(2,1)S(1)}, u32[]{:S(2)}, u32[]{:S(2)}) async-start(bf16[8,40,1024]{2,1,0:T(8,128)(2,1)} %broadcast_in_dim.2), calls=%async_computation.1 | async-start | bytes 1310720 | tf_op jit(solution)/shard_map/all_to_all | solution.py:36
  70.6 2.9 %copy-start.1 = (f32[40,1024]{1,0:T(8,128)S(1)}, f32[40,1024]{1,0:T(8,128)}, u32[]{:S(2)}) copy-start(f32[40,1024]{1,0:T(8,128)} %reduce_sum.30) | copy-start | bytes 491524
  70.6 2.9 %copy-start.2 = (f32[1,40,1024]{2,1,0:T(8,128)S(1)}, f32[1,40,1024]{2,1,0:T(8,128)}, u32[]{:S(2)}) copy-start(f32[1,40,1024]{2,1,0:T(8,128)} %param.6) | copy-start | bytes 491524
where the time goes:
time: 93.7 us; the launch traced here: 91.8 us
  blocking collectives  48.5 us (52%)
  waiting for transfers between devices  16.9 us (18%)
  starting transfers between devices  10.2 us (11%)
  local copies, waits for them, and re-layouts  6.79 us (7%)
  matrix products  4.01 us (4%)
  other arithmetic  3.29 us (4%)
  between operations  2.21 us (2%)
    all_to_all x1, blocking collectives, sent_and_summed(): parts = lax.all_to_all(cut_along(value, dim, size), axis, 0, 0, tiled=True)  39.5 us
    all_to_all x1, waiting for transfers between devices, sent_to_all(): return lax.all_to_all(copies, axis, split_axis=0, concat_axis=0, tiled=True)  14.6 us
    unnamed x1, blocking collectives  8.93 us
    ppermute x1, starting transfers between devices, passed_along(): lax.ppermute(value, axis, [(i, (i + by) % size) for i in range(size)])  6.64 us
    unnamed x12, local copies, waits for them, and re-layouts  4.97 us
    all_to_all x1, starting transfers between devices, sent_to_all(): return lax.all_to_all(copies, axis, split_axis=0, concat_axis=0, tiled=True)  3.54 us
    ppermute x1, waiting for transfers between devices, passed_along(): lax.ppermute(value, axis, [(i, (i + by) % size) for i in range(size)])  2.24 us
    dot_general x1, matrix products, body(): jnp.dot(gathered_copies(normed, 'mp', 0), qkv_matrix, preferred_element_t...  2.07 us
  transfers between devices with their start and end apart: 2, of which 2 were waited for; matrix products, arithmetic and copies ran while one was open for 4% of the time, Pallas kernels for 0%

commit v1 on v0

v1 whole, which is shorter than its diff:
```python
import functools

import jax
import jax.numpy as jnp
from jax import lax
from jax.experimental import pallas as pl
from jax.experimental.pallas import tpu as pltpu
from jax.sharding import PartitionSpec as P

MESH = pl.DeviceIdType.MESH
GROUP = 8


def event_order(ring, groups):
    half = ring // 2
    step, gap, hop, relay = 2.9, 0.7, 3.0, 1.9
    events = []
    for g in range(groups):
        for k in range(1, half):
            events.append((k * step + g * gap, ("sum", k, g)))
        done = half * step + g * gap
        events.append((done, ("finish", half, g)))
        for h in range(1, half + 1):
            events.append((done + hop + (h - 1) * relay, ("pass", h, g)))
    events.sort()
    return [event for _, event in events]


def kernel(
    ring, sections,
    residual_ref, pre_ref, down_ref, gain_ref, qkv_ref, counts_ref,
    finished_ref, out_ref,
    hidden, down, qkv, residual, next_gain, counts, partial, arrived, normed, rows_all,
    load_sem, small_send, small_recv, sum_send, sum_recv, hop_send, hop_recv, pass_send, pass_recv,
):
    me = lax.axis_index("mp")
    sec = lax.axis_index("section")
    half = ring // 2
    rows, width = residual.shape[0], residual.shape[1]
    groups = rows // GROUP
    cut = width // 2
    up, below = lax.rem(me + 1, ring), lax.rem(me + ring - 1, ring)
    after, before = lax.rem(sec + 1, sections), lax.rem(sec + sections - 1, sections)

    order = [half]
    for away in range(half - 1, 0, -1):
        order += [away, ring - away]
    order.append(0)
    loads = {}

    def load(name, src, dst, slot):
        loads[name] = pltpu.make_async_copy(src, dst, load_sem.at[slot])
        loads[name].start()

    def load_rows(r):
        start = pl.multiple_of(lax.rem(me + r, ring) * rows, 8)
        load(r, pre_ref.at[0, pl.ds(start, rows), :], hidden.at[r], r)

    load_rows(order[0])
    load("down", down_ref.at[0], down, ring)
    for r in order[1:]:
        load_rows(r)
    load("residual", residual_ref.at[0], residual, ring + 1)
    load("qkv", qkv_ref, qkv, ring + 2)

    counts[0] = jnp.full(counts.shape[1:], counts_ref[0], jnp.int32)

    barrier = pltpu.get_barrier_semaphore()
    for neighbour in (up, below):
        pl.semaphore_signal(barrier, inc=1, device_id={"mp": neighbour}, device_id_type=MESH)
    for j in range(1, sections):
        other = lax.rem(sec + j, sections)
        pl.semaphore_signal(barrier, inc=1, device_id={"section": other}, device_id_type=MESH)

    def send(src, dst, send_sem, recv_sem, where):
        return pltpu.make_async_remote_copy(
            src_ref=src, dst_ref=dst, send_sem=send_sem, recv_sem=recv_sem,
            device_id=where, device_id_type=MESH,
        )

    def columns(way):
        return pl.ds(way * cut, cut)

    def product(r):
        loads[r].wait()
        acts = jnp.maximum(hidden[r], jnp.zeros((), hidden.dtype))
        made = jnp.dot(acts, down[...], preferred_element_type=jnp.float32)
        partial[r] = made.reshape(groups, GROUP, width)

    sums, passes, hops = {}, {}, {}
    neighbour_of = ({"mp": up}, {"mp": below})

    def start_sum(way, k, g):
        r = half - k if way == 0 else half + k
        src, dst = partial.at[r, g], arrived.at[way, k, g]
        if k == 0:
            src, dst = src.at[:, columns(way)], dst.at[:, columns(way)]
        copy = send(src, dst, sum_send.at[way, k, g], sum_recv.at[way, k, g], neighbour_of[way])
        copy.start()
        sums[way, k, g] = copy

    def start_pass(way, h, g):
        origin = lax.rem(me + (ring - (h - 1) if way == 0 else h - 1), ring)
        block = rows_all.at[origin, g]
        if h == half:
            block = block.at[:, columns(way)]
        copy = send(block, block, pass_send.at[way, h - 1, g], pass_recv.at[way, h - 1, g], neighbour_of[way])
        copy.start()
        passes[way, h, g] = copy

    loads["down"].wait()
    product(half)
    pl.semaphore_wait(barrier, 2 + sections - 1)
    for g in range(groups):
        for way in (0, 1):
            start_sum(way, 0, g)

    small = [send(gain_ref, next_gain, small_send.at[0], small_recv.at[0], {"section": before})]
    for j in range(1, sections):
        where = {"section": lax.rem(sec + j, sections)}
        small.append(send(counts.at[0], counts.at[j], small_send.at[j], small_recv.at[j], where))
    for copy in small:
        copy.start()

    for r in order[1:]:
        product(r)

    finish_ready = []

    def finish(g):
        for way in (0, 1):
            sums[way, half - 1, g].wait_recv()
        if not finish_ready:
            finish_ready.append(True)
            for copy in small:
                copy.wait_recv()
            loads["residual"].wait()
        depth = counts[0]
        for j in range(1, sections):
            depth = depth + counts[j]
        scale = 1.0 / jnp.sqrt(depth.astype(jnp.float32)[:1, :1])
        total = partial[0, g] + arrived[0, half - 1, g] + arrived[1, half - 1, g]
        span = pl.ds(g * GROUP, GROUP)
        stream = residual[span, :] + total * scale
        finished_ref[0, span, :] = stream
        mean_square = jnp.mean(stream * stream, axis=-1, keepdims=True)
        normed[g] = (stream * lax.rsqrt(mean_square + 1e-06) * next_gain[...]).astype(normed.dtype)
        copy = send(normed.at[g], rows_all.at[me, g], hop_send.at[g], hop_recv.at[g], {"section": after})
        copy.start()
        hops[g] = copy

    weights_ready = []

    def project(r):
        if not weights_ready:
            weights_ready.append(True)
            loads["qkv"].wait()
        origin = lax.rem(me + r, ring)
        block = rows_all[origin].astype(jnp.float32).reshape(rows, width).astype(rows_all.dtype)
        made = jnp.dot(block, qkv[...], preferred_element_type=jnp.float32)
        out_ref[origin] = made.astype(out_ref.dtype)

    for name, k, g in event_order(ring, groups):
        if name == "sum":
            for way in (0, 1):
                r = half - k if way == 0 else half + k
                sums[way, k - 1, g].wait_recv()
                if k == 1:
                    at = columns(way)
                    partial[r, g, :, at] = partial[r, g, :, at] + arrived[way, 0, g, :, at]
                else:
                    partial[r, g] = partial[r, g] + arrived[way, k - 1, g]
                start_sum(way, k, g)
        elif name == "finish":
            finish(g)
        else:
            if k == 1:
                hops[g].wait_recv()
                for way in (0, 1):
                    start_pass(way, 1, g)
            else:
                for way in (0, 1):
                    passes[way, k - 1, g].wait_recv()
                    start_pass(way, k, g)
            if g == groups - 1:
                if k == 1:
                    project(0)
                else:
                    project(ring - (k - 1))
                    project(k - 1)

    for g in range(groups):
        for way in (0, 1):
            passes[way, half, g].wait_recv()
    project(half)

    for copies in (small, sums.values(), hops.values(), passes.values()):
        for copy in copies:
            copy.wait_send()


def body(ring, sections, residual_in, pre_activation, down_projection, attention_gain, qkv_projection, layer_counts):
    rows, width = residual_in.shape[1:]
    hidden_units = down_projection.shape[1]
    qkv_matrix = qkv_projection[0].reshape(width, -1)
    out_width = qkv_matrix.shape[1]
    groups, half = rows // GROUP, ring // 2
    any_space = pl.BlockSpec(memory_space=pl.ANY)
    dma = pltpu.SemaphoreType.DMA
    finished, product = pl.pallas_call(
        functools.partial(kernel, ring, sections),
        out_shape=(
            jax.ShapeDtypeStruct(residual_in.shape, jnp.float32),
            jax.ShapeDtypeStruct((ring, rows, out_width), jnp.bfloat16),
        ),
        in_specs=[any_space] * 5 + [pl.BlockSpec(memory_space=pltpu.SMEM)],
        out_specs=(pl.BlockSpec(memory_space=pltpu.VMEM), pl.BlockSpec(memory_space=pltpu.VMEM)),
        scratch_shapes=[
            pltpu.VMEM((ring, rows, hidden_units), jnp.bfloat16),
            pltpu.VMEM((hidden_units, width), jnp.bfloat16),
            pltpu.VMEM((width, out_width), jnp.bfloat16),
            pltpu.VMEM((rows, width), jnp.float32),
            pltpu.VMEM((1, width), jnp.float32),
            pltpu.VMEM((sections, 8, 128), jnp.int32),
            pltpu.VMEM((ring, groups, GROUP, width), jnp.float32),
            pltpu.VMEM((2, half, groups, GROUP, width), jnp.float32),
            pltpu.VMEM((groups, GROUP, width), jnp.bfloat16),
            pltpu.VMEM((ring, groups, GROUP, width), jnp.bfloat16),
            dma((ring + 3,)),
            dma((sections,)),
            dma((sections,)),
            dma((2, half, groups)),
            dma((2, half, groups)),
            dma((groups,)),
            dma((groups,)),
            dma((2, half, groups)),
            dma((2, half, groups)),
        ],
        compiler_params=pltpu.CompilerParams(
            collective_id=0, has_side_effects=True, vmem_limit_bytes=32 * 1024 * 1024
        ),
    )(residual_in, pre_activation, down_projection, attention_gain, qkv_matrix, layer_counts)
    heads, head_width = qkv_projection.shape[2:]
    return finished, product.reshape(1, ring * rows, heads, head_width)


def solution(mesh):
    return jax.shard_map(
        functools.partial(body, mesh.shape["mp"], mesh.shape["section"]),
        mesh=mesh,
        in_specs=(
            P("section", ("dp", "mp"), None),
            P("section", "dp", "mp"),
            P("section", "mp", None),
            P("section", None),
            P("section", None, "mp", None),
            P("section"),
        ),
        out_specs=(P("section", ("dp", "mp"), None), P("section", "dp", "mp", None)),
        check_vma=False,
    )
```

time: 93.7 us -> 53.9 us (0.58)
  the two profiles are of different devices: /device:TPU:1 before, /device:TPU:48 now
where the time goes in v1:
time: 53.9 us; the launch traced here: 53.8 us
  Pallas kernels  48.7 us (90%)
  local copies, waits for them, and re-layouts  3.74 us (7%)
  between operations  1.32 us (2%)
    pallas_call x1, Pallas kernels, body(): pl.pallas_call(functools.partial(kernel, ring, sections), out_shape=(jax....  48.7 us
    unnamed x10, local copies, waits for them, and re-layouts  2.85 us

profile of v1, /device:TPU:48, one launch (start us, length us, event | category | flops | bytes accessed | tf_op | source)
XLA Modules:
  0.0 53.8 jit_solution(7456860088498367003)
XLA Ops:
  1.3 0.0 copy-start
  1.3 0.0 copy-start.1
  1.3 0.0 copy-start.2
  1.3 0.0 copy-start.3
  1.3 1.9 %copy.8 = bf16[128,8,2,384]{3,1,2,0:T(8,128)(2,1)S(1)} copy(bf16[128,8,2,384]{3,2,1,0:T(2,128)(2,1)} %bitcast.4) | data formatting | bytes 3145728
  3.2 0.2 copy-done
  3.3 0.1 copy-done.1
  3.5 0.0 copy-done.2
  3.5 0.0 copy-done.3
  3.5 48.7 %shard_map.77 = (f32[1,40,1024]{2,1,0:T(8,128)S(1)}, bf16[8,40,768]{2,1,0:T(8,128)(2,1)S(1)}) custom-call(f32[1,40,1024]{2,1,0:T(8,128)S(1)} %copy-done.2, bf16[1,320,1024]{2,1,0:T(8,128)(2,1)S(1)} %copy-done.1, bf16[1,1024,1024]{2,1,0:T(8,128)(2,1)S(1)} %copy-done, f32[1,1024]{1,0:T(1,128)S(1)} %copy-done.3, bf16[1024,768]{1,0:T(8,128)(2,1)S(1)} %bitcast.3, ...), custom_call_target="tpu_custom_call" | custom-call | tf_op jit(solution)/shard_map/pallas_call | solution.py:210
  52.2 0.9 %reshape.7 = bf16[1,320,2,384]{3,2,1,0:T(2,128)(2,1)} reshape(bf16[8,40,768]{2,1,0:T(8,128)(2,1)S(1)} %get-tuple-element.5) | data formatting | bytes 983040 | tf_op jit(solution)/shard_map/reshape | solution.py:244
  53.1 0.7 %copy.11 = f32[1,40,1024]{2,1,0:T(8,128)} copy(f32[1,40,1024]{2,1,0:T(8,128)S(1)} %get-tuple-element.8) | data formatting | bytes 327680
Async XLA Ops:
  1.3 2.1 %copy-start = (bf16[1,1024,1024]{2,1,0:T(8,128)(2,1)S(1)}, bf16[1,1024,1024]{2,1,0:T(8,128)(2,1)}, u32[]{:S(2)}) copy-start(bf16[1,1024,1024]{2,1,0:T(8,128)(2,1)} %down_ref.1) | copy-start | bytes 6291460
  1.3 2.2 %copy-start.1 = (bf16[1,320,1024]{2,1,0:T(8,128)(2,1)S(1)}, bf16[1,320,1024]{2,1,0:T(8,128)(2,1)}, u32[]{:S(2)}) copy-start(bf16[1,320,1024]{2,1,0:T(8,128)(2,1)} %pre_ref.1) | copy-start | bytes 1966084
  1.3 2.2 %copy-start.2 = (f32[1,40,1024]{2,1,0:T(8,128)S(1)}, f32[1,40,1024]{2,1,0:T(8,128)}, u32[]{:S(2)}) copy-start(f32[1,40,1024]{2,1,0:T(8,128)} %residual_ref.1) | copy-start | bytes 491524
  1.3 2.2 %copy-start.3 = (f32[1,1024]{1,0:T(1,128)S(1)}, f32[1,1024]{1,0:T(1,128)}, u32[]{:S(2)}) copy-start(f32[1,1024]{1,0:T(1,128)} %gain_ref.1) | copy-start | bytes 12292
